TPU v7x, 32 devices: a whole 2x2x4 slice. The times are simulated.
32 devices in a mesh: sx: 4 (over z), sy: 4 (over y, x), dp: 2 (over core).
Axes of the slice: x: 2, y: 2, z: 4, core: 2. Of those that a mesh axis runs over, the one named last changes fastest.
Arguments:
- features: bfloat16 [2, 32, 32, 4, 8, 128], P('dp', 'sx', 'sy'), may hold values from -6 to 6
- cotangent: bfloat16 [2, 32, 32, 4, 8, 128], P('dp', 'sx', 'sy'), may hold values from -6 to 6
- first_weight: bfloat16 [27, 128, 128], replicated, may hold values from -0.109375 to 0.109375
- second_weight: bfloat16 [27, 128, 128], replicated, may hold values from -0.109375 to 0.109375
- neighbours: int32 [2, 4, 4, 4, 26], P('dp', 'sx', 'sy'), may hold values from -1 to 3, as said below
- counts: int32 [2, 4, 4], P('dp', 'sx', 'sy'), may hold values from 1 to 4, as said below
Outputs:
- out_field: bfloat16 [2, 32, 32, 4, 8, 128], P('dp', 'sx', 'sy')
- grad_input: bfloat16 [2, 32, 32, 4, 8, 128], P('dp', 'sx', 'sy')
- grad_first: float32 [27, 128, 128], replicated
- grad_second: float32 [27, 128, 128], replicated
Inputs may be any that keep to these rules, and one draw needn't show every extreme that they name: Entries name only live slots; slots at or above a column's count have no neighbours; the relation is symmetric: if slot s of column (i, j) names slot t in direction d, then slot t of column (i+dx, j+dy) names s in the opposite direction, and the blocks are adjacent in space; columns outside the grid are never named. `counts`: some column of every workpiece has 4 live slots.
All inputs are finite; a program needn't handle non-finite values.
Results may differ from a plain program's by a relative error of at most 0.012.
Values may be sent and summed in bfloat16 or wider, within the bound.
A program may use at most 192 MiB of HBM per device.

v0:
```python
import functools

import jax
import jax.numpy as jnp
from jax import lax
from jax.experimental import pallas as pl
from jax.experimental.pallas import tpu as pltpu
from jax.sharding import PartitionSpec as P

DIRS = [(dx, dy) for dx in (-1, 0, 1) for dy in (-1, 0, 1) if (dx, dy) != (0, 0)]
F32 = jnp.float32
BF16 = jnp.bfloat16
UNIT = 16


def slope(v):
    s = jax.nn.sigmoid(v)
    return s * (1.0 + v * (1.0 - s))


def kernel(
    nx,
    ny,
    nd,
    feat,
    cot,
    w1,
    w2,
    nb,
    count,
    out_ref,
    gin_ref,
    gw1_ref,
    gw2_ref,
    fld,
    rx,
    ry,
    rc,
    pc_a,
    pc_b,
    pc_c,
    pre,
    gt,
    send_sem,
    recv_sem,
    w1f,
    w2f,
    sel,
    live,
    gb,
    dx_buf,
    hs,
    rb,
    fin,
    pair_send,
    pair_recv,
    rs_send,
    rs_recv,
    ag_send,
    ag_recv,
    fw_send,
    fw_recv,
):
    edge = feat.shape[0]
    rows = feat.shape[2]
    ch = feat.shape[3]
    pairs = edge // 2
    plane = edge * rows
    ix = lax.axis_index("sx")
    iy = lax.axis_index("sy")

    def there(dx, dy):
        ok = None
        for d, i, n in ((dx, ix, nx), (dy, iy, ny)):
            if d == 0:
                continue
            c = (i < n - 1) if d > 0 else (i > 0)
            ok = c if ok is None else jnp.logical_and(ok, c)
        return ok

    def peer(dx, dy):
        px = jnp.minimum(jnp.maximum(ix + dx, 0), nx - 1)
        py = jnp.minimum(jnp.maximum(iy + dy, 0), ny - 1)
        return {"sx": px, "sy": py}

    def halo_ref(f, dx, dy):
        if dy == 0:
            return rx.at[f, (dx + 1) // 2]
        if dx == 0:
            return ry.at[f, (dy + 1) // 2]
        return rc.at[f, (dx + 1) // 2 * 2 + (dy + 1) // 2]

    def desc(f, k):
        dx, dy = DIRS[k]
        far_x = edge - 1 if dx > 0 else 0
        far_y = edge - 1 if dy > 0 else 0
        if dy == 0:
            src = fld.at[f, far_x]
        elif dx == 0:
            src = fld.at[f, :, far_y]
        else:
            src = fld.at[f, far_x, far_y]
        return pltpu.make_async_remote_copy(
            src_ref=src,
            dst_ref=halo_ref(f, -dx, -dy),
            send_sem=send_sem.at[f, k],
            recv_sem=recv_sem.at[f, k],
            device_id=peer(dx, dy),
            device_id_type=pl.DeviceIdType.MESH,
        )

    def send(f):
        for k, (dx, dy) in enumerate(DIRS):
            @pl.when(there(dx, dy))
            def _(k=k):
                desc(f, k).start()

    def arrive(f):
        for k, (dx, dy) in enumerate(DIRS):
            @pl.when(there(-dx, -dy))
            def _(k=k):
                desc(f, k).wait_recv()

    def drain(f):
        for k, (dx, dy) in enumerate(DIRS):
            @pl.when(there(dx, dy))
            def _(k=k):
                desc(f, k).wait_send()

    def put(pc, x, yp, tile):
        t = tile.astype(BF16)
        for b in range(3):
            y = yp - b
            if 0 <= y < edge:
                for c in range(3):
                    lo = (b * 3 + c) * ch
                    pc[x, y, :, lo : lo + ch] = t[c * rows : (c + 1) * rows]

    def line(pc, x, s, tiles):
        cat = jnp.concatenate(tiles, axis=1)
        got = jnp.dot(s, cat, preferred_element_type=F32)
        for y in range(edge):
            put(pc, x, y + 1, got[:, y * ch : (y + 1) * ch])

    def inner(f, pc):
        def body(x, carry):
            line(pc, x + 1, sel[4], [fld[f, x, y] for y in range(edge)])
            return carry

        lax.fori_loop(0, edge, body, 0)

    def outer(f, pc):
        for h in range(2):
            x = 0 if h == 0 else edge + 1
            line(pc, x, sel[6 * h + 1], [rx[f, h, y] for y in range(edge)])
            for g in range(2):
                yp = 0 if g == 0 else edge + 1
                put(pc, x, yp, jnp.dot(sel[6 * h + 2 * g], rc[f, h * 2 + g], preferred_element_type=F32))
            cat = jnp.concatenate([ry[f, h, x] for x in range(edge)], axis=1)
            got = jnp.dot(sel[3 + 2 * h], cat, preferred_element_type=F32)
            for x in range(edge):
                put(pc, x + 1, 0 if h == 0 else edge + 1, got[:, x * ch : (x + 1) * ch])

    def conv(pc, w, use):
        def body(i, carry):
            left = None
            right = None
            for p in range(4):
                lhs = pc[2 * i + p].reshape(plane, 9 * ch)
                wl = w[9 * p : 9 * p + 9].reshape(9 * ch, ch) if p < 3 else None
                wr = w[9 * p - 9 : 9 * p].reshape(9 * ch, ch) if p > 0 else None
                if wr is None:
                    left = jnp.dot(lhs, wl, preferred_element_type=F32)
                elif wl is None:
                    right = right + jnp.dot(lhs, wr, preferred_element_type=F32)
                else:
                    both = jnp.dot(lhs, jnp.concatenate([wl, wr], axis=1), preferred_element_type=F32)
                    left = left + both[:, :ch]
                    right = both[:, ch:] if right is None else right + both[:, ch:]
            use(i, 0, left)
            use(i, 1, right)
            return carry

        lax.fori_loop(0, pairs, body, 0)

    def keep_t(i, h, v):
        gt[h * ch : (h + 1) * ch, pl.ds(pl.multiple_of(i * plane, plane), plane)] = v.T.astype(BF16)

    def tap_out(g, a, b, v):
        per = ch // UNIT
        for c in range(3):
            t = v[:, c * ch : (c + 1) * ch].T.astype(BF16).reshape(per, UNIT, ch)
            gb[g, pl.ds(((a * 3 + b) * 3 + c) * per, per)] = t

    def wgrad(pc, g, lo, hi):
        def body(b, carry):
            lanes = pl.ds(pl.multiple_of(b * (3 * ch), 3 * ch), 3 * ch)
            part = None
            for p in range(4):
                acc = None
                for i in range(pairs):
                    rhs = pc[2 * i + p, :, :, lanes].reshape(plane, 3 * ch)
                    lhs = gt[:, i * plane : (i + 1) * plane]
                    if p == 0:
                        lhs = lhs[:ch]
                    elif p == 3:
                        lhs = lhs[ch:]
                    t = jnp.dot(lhs, rhs, preferred_element_type=F32)
                    acc = t if acc is None else acc + t
                if p == 3:
                    tap_out(g, 2, b, part + acc)
                elif p > 0:
                    tap_out(g, p - 1, b, part + acc[ch:])
                if p < 3:
                    part = acc[:ch]
            return carry

        lax.fori_loop(lo, hi, body, 0)

    n = nx * ny
    units = gb.shape[1]
    half = units // nd
    q = half // n
    core = lax.axis_index("dp")
    me = ix * ny + iy
    mesh_id = pl.DeviceIdType.MESH

    def group(p):
        return {"sx": p // ny, "sy": lax.rem(p, ny)}

    def pair_desc(g):
        return pltpu.make_async_remote_copy(
            src_ref=gb.at[g, pl.ds((1 - core) * half, half)],
            dst_ref=dx_buf.at[g],
            send_sem=pair_send.at[g],
            recv_sem=pair_recv.at[g],
            device_id={"dp": 1 - core},
            device_id_type=mesh_id,
        )

    def rs_desc(g, o):
        p = lax.rem(me + o, n)
        return pltpu.make_async_remote_copy(
            src_ref=hs.at[g, pl.ds(p * q, q)],
            dst_ref=rb.at[g, o],
            send_sem=rs_send.at[g, o],
            recv_sem=rs_recv.at[g, o],
            device_id=group(p),
            device_id_type=mesh_id,
        )

    def ag_desc(g, o, owner):
        here = pl.ds(core * half + owner * q, q)
        return pltpu.make_async_remote_copy(
            src_ref=fin.at[g, here],
            dst_ref=fin.at[g, here],
            send_sem=ag_send.at[g, o],
            recv_sem=ag_recv.at[g, o],
            device_id=group(lax.rem(me + o, n)),
            device_id_type=mesh_id,
        )

    def fw_desc(g, o, side):
        here = pl.ds(side * half + lax.rem(me + n - o, n) * q, q)
        return pltpu.make_async_remote_copy(
            src_ref=fin.at[g, here],
            dst_ref=fin.at[g, here],
            send_sem=fw_send.at[g, o],
            recv_sem=fw_recv.at[g, o],
            device_id={"dp": 1 - core},
            device_id_type=mesh_id,
        )

    def each(lo, hi, fn):
        def body(o, carry):
            fn(o)
            return carry

        lax.fori_loop(lo, hi, body, 0)

    def scatter(g):
        pair_desc(g).wait_recv()

        def one(o):
            p = lax.rem(me + o, n)
            mine = gb[g, pl.ds(core * half + p * q, q)].astype(F32)
            hs[g, pl.ds(p * q, q)] = (mine + dx_buf[g, pl.ds(p * q, q)].astype(F32)).astype(BF16)

        def go(o):
            one(o)
            rs_desc(g, o).start()

        each(1, n, go)
        one(0)

    def gather(g):
        each(1, n, lambda o: rs_desc(g, o).wait_recv())

        def add(o, acc):
            return acc + rb[g, o].astype(F32)

        total = lax.fori_loop(1, n, add, hs[g, pl.ds(me * q, q)].astype(F32))
        fin[g, pl.ds(core * half + me * q, q)] = total.astype(BF16)
        each(1, n, lambda o: ag_desc(g, o, me).start())
        fw_desc(g, 0, core).start()

    def forward(g):
        def one(o):
            ag_desc(g, o, lax.rem(me + n - o, n)).wait_recv()
            fw_desc(g, o, core).start()

        each(1, n, one)

    def finish(g, ref):
        each(0, n, lambda o: fw_desc(g, o, 1 - core).wait_recv())
        ref[...] = fin[g]

    def drain_sums(g):
        pair_desc(g).wait_send()

        def one(o):
            rs_desc(g, o).wait_send()
            ag_desc(g, o, me).wait_send()

        each(1, n, one)
        each(0, n, lambda o: fw_desc(g, o, core).wait_send())

    for dx, dy in DIRS:
        @pl.when(jnp.logical_not(there(dx, dy)))
        def _(dx=dx, dy=dy):
            for f in range(4):
                r = halo_ref(f, dx, dy)
                r[...] = jnp.zeros(r.shape, BF16)

    barrier = pltpu.get_barrier_semaphore()
    each(
        1,
        n,
        lambda o: pl.semaphore_signal(
            barrier, inc=1, device_id=group(lax.rem(me + o, n)), device_id_type=mesh_id
        ),
    )
    pl.semaphore_signal(barrier, inc=1, device_id={"dp": 1 - core}, device_id_type=mesh_id)

    spare = units - 27 * (ch // UNIT)
    if spare:
        for g in range(2):
            gb[g, units - spare :] = jnp.zeros((spare, UNIT, ch), BF16)

    slots = rows // edge
    row = lax.broadcasted_iota(jnp.int32, (plane, ch), 0)
    live[...] = jnp.where(lax.rem(lax.div(row, edge), slots) < count[0], 1.0, 0.0).astype(F32)

    r = lax.broadcasted_iota(jnp.int32, (3 * rows, rows), 0)
    col = lax.broadcasted_iota(jnp.int32, (3 * rows, rows), 1)
    src = lax.rem(r, edge) + lax.div(r, rows) - 1
    dz = jnp.where(src < 0, 0, jnp.where(src >= edge, 2, 1))
    key = dz * slots + lax.rem(lax.div(r, edge), slots)
    same_z = lax.rem(src + edge, edge) == lax.rem(col, edge)
    slot = lax.div(col, edge)
    for d in range(9):
        target = jnp.full((3 * rows, rows), -1, jnp.int32)
        for k in range(3):
            way = d * 3 + k
            for sl in range(slots):
                name = sl if way == 13 else nb[sl, way if way < 13 else way - 1]
                target = jnp.where(key == k * slots + sl, name, target)
        hit = jnp.logical_and(same_z, target == slot)
        sel[d] = jnp.where(hit, 1.0, 0.0).astype(F32).astype(BF16)

    def flip(w, to):
        def body(k, carry):
            to[k] = w[26 - k].astype(F32).T.astype(BF16)
            return carry

        lax.fori_loop(0, 27, body, 0)

    def mask_in(x, carry):
        v = feat[x].astype(F32).reshape(plane, ch) * live[...]
        fld[0, x] = v.astype(BF16).reshape(edge, rows, ch)
        return carry

    lax.fori_loop(0, edge, mask_in, 0)

    pl.semaphore_wait(barrier, n)

    def store(f, x, v):
        fld[f, x] = v.astype(BF16).reshape(edge, rows, ch)

    send(0)
    inner(0, pc_a)
    flip(w2, w2f)
    arrive(0)
    outer(0, pc_a)

    def use1(i, h, v):
        x = 2 * i + h
        pre[x] = v
        store(1, x, v * jax.nn.sigmoid(v) * live[...])

    conv(pc_a, w1, use1)
    send(1)
    inner(1, pc_b)
    flip(w1, w1f)
    arrive(1)
    outer(1, pc_b)

    def use2(i, h, v):
        x = 2 * i + h
        v = v + fld[0, x].reshape(plane, ch).astype(F32)
        s = jax.nn.sigmoid(v)
        out_ref[x] = (v * s * live[...]).astype(BF16).reshape(edge, rows, ch)
        g = cot[x].reshape(plane, ch).astype(F32) * (s * (1.0 + v * (1.0 - s))) * live[...]
        store(2, x, g)
        keep_t(i, h, g)

    conv(pc_b, w2, use2)
    send(2)
    inner(2, pc_c)
    wgrad(pc_b, 0, 0, 3)
    pair_desc(0).start()
    arrive(2)
    outer(2, pc_c)
    scatter(0)

    def use3(i, h, v):
        x = 2 * i + h
        g = v * slope(pre[x]) * live[...]
        store(3, x, g)
        keep_t(i, h, g)

    conv(pc_c, w2f, use3)
    send(3)
    wgrad(pc_a, 1, 0, 2)
    gather(0)
    wgrad(pc_a, 1, 2, 3)
    pair_desc(1).start()
    inner(3, pc_c)
    scatter(1)
    arrive(3)
    outer(3, pc_c)
    forward(0)

    def use4(i, h, v):
        x = 2 * i + h
        g = (fld[2, x].reshape(plane, ch).astype(F32) + v) * live[...]
        gin_ref[x] = g.astype(BF16).reshape(edge, rows, ch)

    conv(pc_c, w1f, use4)
    finish(0, gw2_ref)
    gather(1)
    forward(1)
    finish(1, gw1_ref)
    for f in range(4):
        drain(f)
    drain_sums(0)
    drain_sums(1)


def shards(nx, ny, nd, features, cotangent, first_weight, second_weight, neighbours, counts):
    _, edge, _, slots, _, ch = features.shape
    rows = slots * edge
    plane = edge * rows
    flat = (edge, edge, rows, ch)
    scale = float(nx * ny * nd * slots * edge**3) ** -0.5
    vmem = pl.BlockSpec(memory_space=pltpu.VMEM)
    smem = pl.BlockSpec(memory_space=pltpu.SMEM)
    n = nx * ny
    q = -(-27 * ch // (UNIT * n * nd))
    units = q * n * nd
    gshape = jax.ShapeDtypeStruct((units, UNIT, ch), BF16)
    fshape = jax.ShapeDtypeStruct(flat, BF16)
    out, gin, g1, g2 = pl.pallas_call(
        functools.partial(kernel, nx, ny, nd),
        out_shape=[fshape, fshape, gshape, gshape],
        in_specs=[vmem] * 4 + [smem] * 2,
        out_specs=[vmem] * 4,
        scratch_shapes=[
            pltpu.VMEM((4,) + flat, BF16),
            pltpu.VMEM((4, 2, edge, rows, ch), BF16),
            pltpu.VMEM((4, 2, edge, rows, ch), BF16),
            pltpu.VMEM((4, 4, rows, ch), BF16),
            pltpu.VMEM((edge + 2, edge, rows, 9 * ch), BF16),
            pltpu.VMEM((edge + 2, edge, rows, 9 * ch), BF16),
            pltpu.VMEM((edge + 2, edge, rows, 9 * ch), BF16),
            pltpu.VMEM((edge, plane, ch), F32),
            pltpu.VMEM((2 * ch, edge // 2 * plane), BF16),
            pltpu.SemaphoreType.DMA((4, len(DIRS))),
            pltpu.SemaphoreType.DMA((4, len(DIRS))),
            pltpu.VMEM((27, ch, ch), BF16),
            pltpu.VMEM((27, ch, ch), BF16),
            pltpu.VMEM((9, 3 * rows, rows), BF16),
            pltpu.VMEM((plane, ch), F32),
            pltpu.VMEM((2, units, UNIT, ch), BF16),
            pltpu.VMEM((2, units // nd, UNIT, ch), BF16),
            pltpu.VMEM((2, units // nd, UNIT, ch), BF16),
            pltpu.VMEM((2, n, q, UNIT, ch), BF16),
            pltpu.VMEM((2, units, UNIT, ch), BF16),
        ]
        + [pltpu.SemaphoreType.DMA((2,))] * 2
        + [pltpu.SemaphoreType.DMA((2, n))] * 6,
        compiler_params=pltpu.CompilerParams(
            collective_id=0, has_side_effects=True, vmem_limit_bytes=60 * 1024 * 1024
        ),
    )(
        features.reshape(flat),
        cotangent.reshape(flat),
        first_weight,
        second_weight,
        neighbours[0, 0, 0],
        counts.reshape(1),
    )
    def finish(g):
        g = g.reshape(-1, ch)[: 27 * ch]
        return g.reshape(27, ch, ch).astype(F32) * scale

    return out.reshape(features.shape), gin.reshape(features.shape), finish(g1), finish(g2)


def solution(mesh):
    field = P("dp", "sx", "sy", None, None, None)
    return jax.shard_map(
        functools.partial(shards, mesh.shape["sx"], mesh.shape["sy"], mesh.shape["dp"]),
        mesh=mesh,
        in_specs=(field, field, P(), P(), P("dp", "sx", "sy", None, None), P("dp", "sx", "sy")),
        out_specs=(field, field, P(), P()),
        check_vma=False,
    )
```

profile of v0, /device:TPU:29, one launch (start us, length us, event | category | flops | bytes accessed | tf_op | source)
XLA Modules:
  0.0 86.5 jit_solution(16873384484820189207)
XLA Ops:
  1.3 80.0 %shard_map.93 = (bf16[8,8,32,128]{3,2,1,0:T(8,128)(2,1)}, bf16[8,8,32,128]{3,2,1,0:T(8,128)(2,1)}, bf16[224,16,128]{2,1,0:T(8,128)(2,1)}, bf16[224,16,128]{2,1,0:T(8,128)(2,1)}) custom-call(bf16[8,8,32,128]{3,2,1,0:T(8,128)(2,1)} %bitcast.13, bf16[8,8,32,128]{3,2,1,0:T(8,128)(2,1)} %bitcast.14, bf16[27,128,128]{2,1,0:T(8,128)(2,1)} %w1.1, ...), custom_call_target="tpu_custom_call" | custom-call | tf_op jit(solution)/shard_map/pallas_call | solution.py:473
  81.3 0.0 copy-start.1
  81.3 0.0 copy-start
  81.4 3.6 %convert_multiply_fusion = (f32[216,16,128]{2,1,0:T(8,128)}, f32[216,16,128]{2,1,0:T(8,128)}) fusion(bf16[224,16,128]{2,1,0:T(8,128)(2,1)} %get-tuple-element.11, bf16[224,16,128]{2,1,0:T(8,128)(2,1)} %get-tuple-element.10), kind=kLoop, calls=%fused_computation | loop fusion | flops 1769472 | bytes 5308416 | tf_op jit(solution)/shard_map/mul | solution.py:515
  84.9 0.0 copy-done.1
  84.9 0.8 copy.13
  85.7 0.0 copy-done
  85.7 0.8 copy.14
Async XLA Ops:
  81.3 3.6 %copy-start.1 = (bf16[8,8,32,128]{3,2,1,0:T(8,128)(2,1)S(1)}, bf16[8,8,32,128]{3,2,1,0:T(8,128)(2,1)}, u32[]{:S(2)}) copy-start(bf16[8,8,32,128]{3,2,1,0:T(8,128)(2,1)} %get-tuple-element.8) | copy-start | bytes 1572868
  81.3 4.4 %copy-start = (bf16[8,8,32,128]{3,2,1,0:T(8,128)(2,1)S(1)}, bf16[8,8,32,128]{3,2,1,0:T(8,128)(2,1)}, u32[]{:S(2)}) copy-start(bf16[8,8,32,128]{3,2,1,0:T(8,128)(2,1)} %get-tuple-element.9) | copy-start | bytes 1572868
where the time goes:
time: 86.7 us; the launch traced here: 86.5 us
  Pallas kernels  80 us (92%)
  other arithmetic  3.59 us (4%)
  local copies, waits for them, and re-layouts  1.59 us (2%)
  between operations  1.3 us (1%)
    pallas_call x1, Pallas kernels, shards(): pl.pallas_call(functools.partial(kernel, nx, ny, nd), out_shape=[fshape,...  80 us
    mul x1, other arithmetic, finish(): return g.reshape(27, ch, ch).astype(F32) * scale  3.59 us

commit v1 on v0

--- a/solution.py
+++ b/solution.py
@@ -16,6 +16,54 @@
 def slope(v):
     s = jax.nn.sigmoid(v)
     return s * (1.0 + v * (1.0 - s))
+
+
+MODES = (("abz", False), ("yz", True))
+
+
+def side_of(ny):
+    f = 1
+    while f * f < ny:
+        f += 1
+    return f if f * f == ny else None
+
+
+def layout(nx, ny, nd, ch):
+    n = nx * ny
+    per = 9 * ch // UNIT
+    total = -(-3 * per // (n * nd))
+    pieces = []
+    sems = 0
+    room = 0
+    for g in range(2):
+        mode, whole = MODES[g]
+        f = side_of(ny)
+        sizes = (f, f, nx) if mode == "abz" and f else (ny, nx)
+        done = 0
+        for b in range(3):
+            upto = total if b == 2 else min((b + 1) * per // (n * nd), total)
+            q = upto - done
+            if q <= 0:
+                continue
+            item = dict(g=g, b=b, q=q, base=done * n * nd, sizes=sizes, whole=whole, rs=[], ag=[], slot=[])
+            item["pair"] = sems
+            sems += 1
+            left = n * q
+            for l, s in enumerate(sizes):
+                last = whole and l == len(sizes) - 1
+                step = left if last else left // s
+                item["rs"].append(sems)
+                sems += s
+                item["ag"].append(sems)
+                sems += 0 if last else s
+                item["slot"].append((room, step))
+                room += s * step
+                left = left // s
+            item["fw"] = sems
+            sems += sizes[0]
+            pieces.append(item)
+            done = upto
+    return pieces, sems, room, total * n * nd
 
 
 def kernel(
@@ -52,14 +100,8 @@
     hs,
     rb,
     fin,
-    pair_send,
-    pair_recv,
-    rs_send,
-    rs_recv,
-    ag_send,
-    ag_recv,
-    fw_send,
-    fw_recv,
+    sum_send,
+    sum_recv,
 ):
     edge = feat.shape[0]
     rows = feat.shape[2]
@@ -161,7 +203,7 @@
             for x in range(edge):
                 put(pc, x + 1, 0 if h == 0 else edge + 1, got[:, x * ch : (x + 1) * ch])
 
-    def conv(pc, w, use):
+    def conv(pc, w, use, hooks=None):
         def body(i, carry):
             left = None
             right = None
@@ -179,6 +221,7 @@
                     right = both[:, ch:] if right is None else right + both[:, ch:]
             use(i, 0, left)
             use(i, 1, right)
+            hooked(i, hooks)
             return carry
 
         lax.fori_loop(0, pairs, body, 0)
@@ -190,9 +233,16 @@
         per = ch // UNIT
         for c in range(3):
             t = v[:, c * ch : (c + 1) * ch].T.astype(BF16).reshape(per, UNIT, ch)
-            gb[g, pl.ds(((a * 3 + b) * 3 + c) * per, per)] = t
-
-    def wgrad(pc, g, lo, hi):
+            gb[g, pl.ds(((b * 3 + a) * 3 + c) * per, per)] = t
+
+    def hooked(i, hooks):
+        for at, fns in sorted((hooks or {}).items()):
+            @pl.when(i == at)
+            def _(fns=fns):
+                for fn in fns:
+                    fn()
+
+    def wgrad(pc, g, hooks):
         def body(b, carry):
             lanes = pl.ds(pl.multiple_of(b * (3 * ch), 3 * ch), 3 * ch)
             part = None
@@ -213,117 +263,240 @@
                     tap_out(g, p - 1, b, part + acc[ch:])
                 if p < 3:
                     part = acc[:ch]
+            hooked(b, hooks)
             return carry
 
-        lax.fori_loop(lo, hi, body, 0)
+        lax.fori_loop(0, 3, body, 0)
 
     n = nx * ny
-    units = gb.shape[1]
-    half = units // nd
-    q = half // n
     core = lax.axis_index("dp")
     me = ix * ny + iy
     mesh_id = pl.DeviceIdType.MESH
-
-    def group(p):
-        return {"sx": p // ny, "sy": lax.rem(p, ny)}
-
-    def pair_desc(g):
-        return pltpu.make_async_remote_copy(
-            src_ref=gb.at[g, pl.ds((1 - core) * half, half)],
-            dst_ref=dx_buf.at[g],
-            send_sem=pair_send.at[g],
-            recv_sem=pair_recv.at[g],
-            device_id={"dp": 1 - core},
-            device_id_type=mesh_id,
-        )
-
-    def rs_desc(g, o):
-        p = lax.rem(me + o, n)
-        return pltpu.make_async_remote_copy(
-            src_ref=hs.at[g, pl.ds(p * q, q)],
-            dst_ref=rb.at[g, o],
-            send_sem=rs_send.at[g, o],
-            recv_sem=rs_recv.at[g, o],
-            device_id=group(p),
-            device_id_type=mesh_id,
-        )
-
-    def ag_desc(g, o, owner):
-        here = pl.ds(core * half + owner * q, q)
-        return pltpu.make_async_remote_copy(
-            src_ref=fin.at[g, here],
-            dst_ref=fin.at[g, here],
-            send_sem=ag_send.at[g, o],
-            recv_sem=ag_recv.at[g, o],
-            device_id=group(lax.rem(me + o, n)),
-            device_id_type=mesh_id,
-        )
-
-    def fw_desc(g, o, side):
-        here = pl.ds(side * half + lax.rem(me + n - o, n) * q, q)
-        return pltpu.make_async_remote_copy(
-            src_ref=fin.at[g, here],
-            dst_ref=fin.at[g, here],
-            send_sem=fw_send.at[g, o],
-            recv_sem=fw_recv.at[g, o],
-            device_id={"dp": 1 - core},
-            device_id_type=mesh_id,
-        )
+    pieces, _, _, units = layout(nx, ny, nd, ch)
+    side = side_of(ny)
 
     def each(lo, hi, fn):
+        if hi - lo <= 3:
+            for o in range(lo, hi):
+                fn(o)
+            return
+
         def body(o, carry):
             fn(o)
             return carry
 
         lax.fori_loop(lo, hi, body, 0)
 
-    def scatter(g):
-        pair_desc(g).wait_recv()
-
-        def one(o):
-            p = lax.rem(me + o, n)
-            mine = gb[g, pl.ds(core * half + p * q, q)].astype(F32)
-            hs[g, pl.ds(p * q, q)] = (mine + dx_buf[g, pl.ds(p * q, q)].astype(F32)).astype(BF16)
-
-        def go(o):
-            one(o)
-            rs_desc(g, o).start()
-
-        each(1, n, go)
-        one(0)
-
-    def gather(g):
-        each(1, n, lambda o: rs_desc(g, o).wait_recv())
-
-        def add(o, acc):
-            return acc + rb[g, o].astype(F32)
-
-        total = lax.fori_loop(1, n, add, hs[g, pl.ds(me * q, q)].astype(F32))
-        fin[g, pl.ds(core * half + me * q, q)] = total.astype(BF16)
-        each(1, n, lambda o: ag_desc(g, o, me).start())
-        fw_desc(g, 0, core).start()
-
-    def forward(g):
-        def one(o):
-            ag_desc(g, o, lax.rem(me + n - o, n)).wait_recv()
-            fw_desc(g, o, core).start()
-
-        each(1, n, one)
+    def group(p):
+        return {"sx": p // ny, "sy": lax.rem(p, ny)}
+
+    class Sum:
+        def __init__(self, item):
+            self.it = item
+            self.g = item["g"]
+            q = item["q"]
+            self.sizes = item["sizes"]
+            m = self.m = len(self.sizes)
+            if m == 3:
+                cx = lax.rem(iy, side)
+                cy = lax.div(iy, side)
+                first = cx + core * (cy - cx)
+                second = cx + cy - first
+                self.coords = (first, second, ix)
+                self.other = second
+                self.steps = (1 + core * (side - 1), side - core * (side - 1))
+            else:
+                self.coords = (iy, ix)
+                self.other = iy
+                self.steps = (1,)
+            self.size = [n * q]
+            self.off = [0]
+            for l in range(m):
+                self.size.append(self.size[-1] // self.sizes[l])
+                self.off.append(self.off[-1] + self.coords[l] * self.size[-1])
+            self.hb = item["base"] // nd
+            self.mine = item["base"] + core * (n * q)
+            self.theirs = item["base"] + (1 - core) * (n * q)
+            self.whole = item["whole"]
+
+        def to(self, l, o):
+            c = self.coords[l]
+            p = lax.rem(c + o, self.sizes[l])
+            if l == self.m - 1:
+                return p, {"sx": p}
+            return p, {"sy": iy + (p - c) * self.steps[l]}
+
+        def frm(self, l, o):
+            return lax.rem(self.coords[l] + self.sizes[l] - o, self.sizes[l])
+
+        def copy(self, src, dst, k, dev):
+            return pltpu.make_async_remote_copy(
+                src_ref=src,
+                dst_ref=dst,
+                send_sem=sum_send.at[k],
+                recv_sem=sum_recv.at[k],
+                device_id=dev,
+                device_id_type=mesh_id,
+            )
+
+        def pair(self):
+            return self.copy(
+                gb.at[self.g, pl.ds(self.theirs, self.size[0])],
+                dx_buf.at[self.g, pl.ds(self.hb, self.size[0])],
+                self.it["pair"],
+                {"dp": 1 - core},
+            )
+
+        def last(self, l):
+            return self.whole and l == self.m - 1
+
+        def rs(self, l, o):
+            p, dev = self.to(l, o)
+            room, step = self.it["slot"][l]
+            at = self.off[l] if self.last(l) else self.off[l] + p * step
+            return self.copy(
+                hs.at[self.g, pl.ds(self.hb + at, step)],
+                rb.at[pl.ds(room + o * step, step)],
+                self.it["rs"][l] + o,
+                dev,
+            )
+
+        def ag(self, l, o, owner):
+            _, dev = self.to(l, o)
+            size = self.size[l + 1]
+            here = pl.ds(self.mine + self.off[l] + owner * size, size)
+            return self.copy(fin.at[self.g, here], fin.at[self.g, here], self.it["ag"][l] + o, dev)
+
+        def fw(self, o, base, c):
+            size = self.size[1]
+            here = pl.ds(base + lax.rem(c + self.sizes[0] - o, self.sizes[0]) * size, size)
+            return self.copy(fin.at[self.g, here], fin.at[self.g, here], self.it["fw"] + o, {"dp": 1 - core})
+
+        def begin(self):
+            self.pair().start()
+
+        def total(self, l, at, size):
+            own = hs[self.g, pl.ds(self.hb + at, size)] if l >= 0 else gb[self.g, pl.ds(self.mine + at, size)]
+            v = own.astype(F32)
+            if l < 0:
+                return v + dx_buf[self.g, pl.ds(self.hb + at, size)].astype(F32)
+            room, step = self.it["slot"][l]
+            back = at - self.off[l + 1]
+
+            def add(o, acc):
+                return acc + rb[pl.ds(room + o * step + back, size)].astype(F32)
+
+            if self.sizes[l] <= 4:
+                for o in range(1, self.sizes[l]):
+                    v = add(o, v)
+                return v
+            return lax.fori_loop(1, self.sizes[l], add, v)
+
+        def reduce(self, l):
+            if l < 0:
+                self.pair().wait_recv()
+            else:
+                each(1, self.sizes[l], lambda o: self.rs(l, o).wait_recv())
+            nxt = l + 1
+            if nxt == self.m:
+                size = self.size[self.m]
+                v = self.total(l, self.off[self.m], size)
+                fin[self.g, pl.ds(self.mine + self.off[self.m], size)] = v.astype(BF16)
+                self.share(l)
+                return
+            room, step = self.it["slot"][nxt]
+            if self.last(nxt):
+                v = self.total(l, self.off[nxt], step).astype(BF16)
+                hs[self.g, pl.ds(self.hb + self.off[nxt], step)] = v
+                rb[pl.ds(room, step)] = v
+                each(1, self.sizes[nxt], lambda o: self.rs(nxt, o).start())
+                return
+
+            def one(o):
+                at = self.off[nxt] + lax.rem(self.coords[nxt] + o, self.sizes[nxt]) * step
+                hs[self.g, pl.ds(self.hb + at, step)] = self.total(l, at, step).astype(BF16)
+
+            def go(o):
+                one(o)
+                self.rs(nxt, o).start()
+
+            each(1, self.sizes[nxt], go)
+            one(0)
+
+        def settle(self):
+            l = self.m - 1
+            each(1, self.sizes[l], lambda o: self.rs(l, o).wait_recv())
+            room, step = self.it["slot"][l]
+
+            def part(p):
+                return rb[pl.ds(room + self.frm(l, p) * step, step)].astype(F32)
+
+            v = part(0)
+            if self.sizes[l] <= 4:
+                for p in range(1, self.sizes[l]):
+                    v = v + part(p)
+            else:
+                v = lax.fori_loop(1, self.sizes[l], lambda p, acc: acc + part(p), v)
+            fin[self.g, pl.ds(self.mine + self.off[l], step)] = v.astype(BF16)
+            self.share(l - 1)
+
+        def share(self, l):
+            each(1, self.sizes[l], lambda o: self.ag(l, o, self.coords[l]).start())
+            if l == 0:
+                self.fw(0, self.mine, self.coords[0]).start()
+
+        def gather(self, l):
+            def one(o):
+                self.ag(l, o, self.frm(l, o)).wait_recv()
+                if l == 0:
+                    self.fw(o, self.mine, self.coords[0]).start()
+
+            each(1, self.sizes[l], one)
+            if l > 0:
+                self.share(l - 1)
+
+        def arrive(self):
+            each(0, self.sizes[0], lambda o: self.fw(o, self.theirs, self.other).wait_recv())
+
+        def stages(self):
+            out = [self.begin]
+            for l in range(-1, self.m - (1 if self.whole else 0)):
+                out.append(functools.partial(self.reduce, l))
+            if self.whole:
+                out.append(self.settle)
+            for l in reversed(range(self.m - (1 if self.whole else 0))):
+                out.append(functools.partial(self.gather, l))
+            out.append(self.arrive)
+            return out
+
+        def drain(self):
+            self.pair().wait_send()
+            for l in range(self.m):
+                each(1, self.sizes[l], lambda o: self.rs(l, o).wait_send())
+                if not self.last(l):
+                    each(1, self.sizes[l], lambda o: self.ag(l, o, self.coords[l]).wait_send())
+            each(0, self.sizes[0], lambda o: self.fw(o, self.mine, self.coords[0]).wait_send())
+
+    sums = [Sum(item) for item in pieces]
+    queue = {(s.g, s.it["b"]): s.stages() for s in sums}
+
+    listed = set()
+
+    def adv(g, b, s):
+        listed.add((g, b, s))
+
+        def run():
+            if s < len(queue.get((g, b), [])):
+                queue[g, b][s]()
+
+        return run
 
     def finish(g, ref):
-        each(0, n, lambda o: fw_desc(g, o, 1 - core).wait_recv())
-        ref[...] = fin[g]
-
-    def drain_sums(g):
-        pair_desc(g).wait_send()
-
-        def one(o):
-            rs_desc(g, o).wait_send()
-            ag_desc(g, o, me).wait_send()
-
-        each(1, n, one)
-        each(0, n, lambda o: fw_desc(g, o, core).wait_send())
+        per = ch // UNIT
+        for k in range(27):
+            a, b, c = k // 9, k // 3 % 3, k % 3
+            j = (b * 3 + a) * 3 + c
+            ref[k * per : (k + 1) * per] = fin[g, j * per : (j + 1) * per]
 
     for dx, dy in DIRS:
         @pl.when(jnp.logical_not(there(dx, dy)))
@@ -414,14 +587,38 @@
         store(2, x, g)
         keep_t(i, h, g)
 
+    AT = {
+        "w2": {0: [adv(0, 0, 0)], 1: [adv(0, 1, 0), adv(0, 0, 1)], 2: [adv(0, 2, 0), adv(0, 1, 1)]},
+        "o2": [adv(0, 2, 1)],
+        "c3": {
+            0: [adv(0, 0, 2)],
+            1: [adv(0, 1, 2)],
+            2: [adv(0, 2, 2), adv(0, 0, 3)],
+            3: [adv(0, 1, 3)],
+        },
+        "w1": {
+            0: [adv(1, 0, 0), adv(0, 2, 3)],
+            1: [adv(1, 1, 0), adv(1, 0, 1), adv(0, 0, 4), adv(0, 1, 4)],
+            2: [adv(1, 2, 0), adv(1, 1, 1), adv(0, 2, 4)],
+        },
+        "o3": [adv(1, 2, 1), adv(1, 0, 2)],
+        "c4": {
+            0: [adv(1, 1, 2), adv(0, 0, 5)],
+            1: [adv(1, 2, 2), adv(0, 1, 5)],
+            2: [adv(0, 2, 5), adv(0, 0, 6), adv(1, 0, 3)],
+            3: [adv(0, 1, 6), adv(0, 2, 6), adv(1, 1, 3)],
+        },
+        "end": [adv(0, 0, 7), adv(0, 1, 7), adv(1, 2, 3), adv(1, 0, 4), adv(0, 2, 7), adv(1, 1, 4), adv(0, 0, 8), adv(1, 2, 4)],
+    }
+
     conv(pc_b, w2, use2)
     send(2)
     inner(2, pc_c)
-    wgrad(pc_b, 0, 0, 3)
-    pair_desc(0).start()
+    wgrad(pc_b, 0, AT["w2"])
     arrive(2)
     outer(2, pc_c)
-    scatter(0)
+    for fn in AT["o2"]:
+        fn()
 
     def use3(i, h, v):
         x = 2 * i + h
@@ -429,32 +626,33 @@
         store(3, x, g)
         keep_t(i, h, g)
 
-    conv(pc_c, w2f, use3)
+    conv(pc_c, w2f, use3, AT["c3"])
     send(3)
-    wgrad(pc_a, 1, 0, 2)
-    gather(0)
-    wgrad(pc_a, 1, 2, 3)
-    pair_desc(1).start()
+    wgrad(pc_a, 1, AT["w1"])
     inner(3, pc_c)
-    scatter(1)
     arrive(3)
     outer(3, pc_c)
-    forward(0)
+    for fn in AT["o3"]:
+        fn()
 
     def use4(i, h, v):
         x = 2 * i + h
         g = (fld[2, x].reshape(plane, ch).astype(F32) + v) * live[...]
         gin_ref[x] = g.astype(BF16).reshape(edge, rows, ch)
 
-    conv(pc_c, w1f, use4)
+    conv(pc_c, w1f, use4, AT["c4"])
+    for fn in AT["end"]:
+        fn()
+    for k, todo in queue.items():
+        for s, fn in enumerate(todo):
+            if k + (s,) not in listed:
+                fn()
     finish(0, gw2_ref)
-    gather(1)
-    forward(1)
     finish(1, gw1_ref)
     for f in range(4):
         drain(f)
-    drain_sums(0)
-    drain_sums(1)
+    for s in sums:
+        s.drain()
 
 
 def shards(nx, ny, nd, features, cotangent, first_weight, second_weight, neighbours, counts):
@@ -465,9 +663,7 @@
     scale = float(nx * ny * nd * slots * edge**3) ** -0.5
     vmem = pl.BlockSpec(memory_space=pltpu.VMEM)
     smem = pl.BlockSpec(memory_space=pltpu.SMEM)
-    n = nx * ny
-    q = -(-27 * ch // (UNIT * n * nd))
-    units = q * n * nd
+    _, nsem, room, units = layout(nx, ny, nd, ch)
     gshape = jax.ShapeDtypeStruct((units, UNIT, ch), BF16)
     fshape = jax.ShapeDtypeStruct(flat, BF16)
     out, gin, g1, g2 = pl.pallas_call(
@@ -494,11 +690,11 @@
             pltpu.VMEM((2, units, UNIT, ch), BF16),
             pltpu.VMEM((2, units // nd, UNIT, ch), BF16),
             pltpu.VMEM((2, units // nd, UNIT, ch), BF16),
-            pltpu.VMEM((2, n, q, UNIT, ch), BF16),
+            pltpu.VMEM((room, UNIT, ch), BF16),
             pltpu.VMEM((2, units, UNIT, ch), BF16),
-        ]
-        + [pltpu.SemaphoreType.DMA((2,))] * 2
-        + [pltpu.SemaphoreType.DMA((2, n))] * 6,
+            pltpu.SemaphoreType.DMA((nsem,)),
+            pltpu.SemaphoreType.DMA((nsem,)),
+        ],
         compiler_params=pltpu.CompilerParams(
             collective_id=0, has_side_effects=True, vmem_limit_bytes=60 * 1024 * 1024
         ),

time: 86.7 us -> 72 us (0.83)
  the two profiles are of different devices: /device:TPU:29 before, /device:TPU:1 now
where the time goes in v1:
time: 72 us; the launch traced here: 71.8 us
  Pallas kernels  65.3 us (91%)
  other arithmetic  3.59 us (5%)
  local copies, waits for them, and re-layouts  1.59 us (2%)
  between operations  1.3 us (2%)
    pallas_call x1, Pallas kernels, shards(): pl.pallas_call(functools.partial(kernel, nx, ny, nd), out_shape=[fshape,...  65.3 us
    mul x1, other arithmetic, finish(): return g.reshape(27, ch, ch).astype(F32) * scale  3.59 us
    unnamed x6, local copies, waits for them, and re-layouts  1.59 us

profile of v1, /device:TPU:1, one launch (start us, length us, event | category | flops | bytes accessed | tf_op | source)
XLA Modules:
  0.0 71.8 jit_solution(6392263803952998982)
XLA Ops:
  1.3 65.3 %shard_map.93 = (bf16[8,8,32,128]{3,2,1,0:T(8,128)(2,1)}, bf16[8,8,32,128]{3,2,1,0:T(8,128)(2,1)}, bf16[224,16,128]{2,1,0:T(8,128)(2,1)}, bf16[224,16,128]{2,1,0:T(8,128)(2,1)}) custom-call(bf16[8,8,32,128]{3,2,1,0:T(8,128)(2,1)} %bitcast.13, bf16[8,8,32,128]{3,2,1,0:T(8,128)(2,1)} %bitcast.14, bf16[27,128,128]{2,1,0:T(8,128)(2,1)} %w1.1, ...), custom_call_target="tpu_custom_call" | custom-call | tf_op jit(solution)/shard_map/pallas_call | solution.py:669
  66.6 0.0 copy-start.1
  66.6 0.0 copy-start
  66.6 3.6 %convert_multiply_fusion = (f32[216,16,128]{2,1,0:T(8,128)}, f32[216,16,128]{2,1,0:T(8,128)}) fusion(bf16[224,16,128]{2,1,0:T(8,128)(2,1)} %get-tuple-element.11, bf16[224,16,128]{2,1,0:T(8,128)(2,1)} %get-tuple-element.10), kind=kLoop, calls=%fused_computation | loop fusion | flops 1769472 | bytes 5308416 | tf_op jit(solution)/shard_map/mul | solution.py:711
  70.2 0.0 copy-done.1
  70.2 0.8 %copy.13 = bf16[1,8,8,4,8,128]{5,4,3,2,1,0:T(8,128)(2,1)} copy(bf16[1,8,8,4,8,128]{5,4,3,2,1,0:T(8,128)(2,1)S(1)} %bitcast.12) | data formatting | bytes 1048576
  71.0 0.0 copy-done
  71.0 0.8 %copy.14 = bf16[1,8,8,4,8,128]{5,4,3,2,1,0:T(8,128)(2,1)} copy(bf16[1,8,8,4,8,128]{5,4,3,2,1,0:T(8,128)(2,1)S(1)} %bitcast.11) | data formatting | bytes 1048576
Async XLA Ops:
  66.6 3.6 %copy-start.1 = (bf16[8,8,32,128]{3,2,1,0:T(8,128)(2,1)S(1)}, bf16[8,8,32,128]{3,2,1,0:T(8,128)(2,1)}, u32[]{:S(2)}) copy-start(bf16[8,8,32,128]{3,2,1,0:T(8,128)(2,1)} %get-tuple-element.8) | copy-start | bytes 1572868
  66.6 4.4 %copy-start = (bf16[8,8,32,128]{3,2,1,0:T(8,128)(2,1)S(1)}, bf16[8,8,32,128]{3,2,1,0:T(8,128)(2,1)}, u32[]{:S(2)}) copy-start(bf16[8,8,32,128]{3,2,1,0:T(8,128)(2,1)} %get-tuple-element.9) | copy-start | bytes 1572868

commit v2 on v1

--- a/solution.py
+++ b/solution.py
@@ -18,7 +18,22 @@
     return s * (1.0 + v * (1.0 - s))
 
 
-MODES = (("abz", False), ("yz", True))
+MODES = (
+    ("yz", "yz", "yz", "yz", "yz"),
+    ("yz", "yz", "yzw", "yzw", "yzw"),
+)
+STEPS = {
+    (0, 0): ("w2.0", "w2.2", "c3.3", "w1.4", "c4.2",),
+    (0, 1): ("w2.1", "w2.3", "c3.3", "w1.4", "c4.2",),
+    (0, 2): ("w2.2", "w2.4", "c3.3", "w1.4", "c4.2",),
+    (0, 3): ("w2.3", "o2", "w1.0", "o3", "c4.2",),
+    (0, 4): ("w2.4", "c3.0", "w1.1", "o3", "c4.2",),
+    (1, 0): ("w1.0", "w1.2", "c4.1",),
+    (1, 1): ("w1.1", "w1.3", "c4.1",),
+    (1, 2): ("w1.2", "w1.4", "c4.1",),
+    (1, 3): ("w1.3", "o3", "c4.3",),
+    (1, 4): ("w1.4", "o3", "c4.3",),
+}
 
 
 def side_of(ny):
@@ -30,56 +45,82 @@
 
 def layout(nx, ny, nd, ch):
     n = nx * ny
-    per = 9 * ch // UNIT
-    total = -(-3 * per // (n * nd))
+    total = -(-27 * ch // (UNIT * n * nd))
     pieces = []
     sems = 0
     room = 0
+    out = {}
+
+    def sent(g, kind, count):
+        out[g, kind] = out.get((g, kind), 0) + count
+
     for g in range(2):
-        mode, whole = MODES[g]
         f = side_of(ny)
-        sizes = (f, f, nx) if mode == "abz" and f else (ny, nx)
         done = 0
-        for b in range(3):
-            upto = total if b == 2 else min((b + 1) * per // (n * nd), total)
+        for b in range(5):
+            upto = total if b == 4 else min((b + 1) * (6 * ch // UNIT) // (n * nd), total)
             q = upto - done
             if q <= 0:
                 continue
+            mode = MODES[g][b]
+            whole = mode[-1] == "w"
+            if mode == "all":
+                sizes = (n,)
+            elif mode[:3] == "abz" and f:
+                sizes = (f, f, nx)
+            else:
+                sizes = (ny, nx)
             item = dict(g=g, b=b, q=q, base=done * n * nd, sizes=sizes, whole=whole, rs=[], ag=[], slot=[])
             item["pair"] = sems
             sems += 1
             left = n * q
+            sent(g, "pair", left)
             for l, s in enumerate(sizes):
                 last = whole and l == len(sizes) - 1
                 step = left if last else left // s
                 item["rs"].append(sems)
-                sems += s
+                sems += 1
+                sent(g, "rs", (s - 1) * step)
                 item["ag"].append(sems)
-                sems += 0 if last else s
+                if l == 0:
+                    sems += s
+                elif not last:
+                    sems += 1
+                if not last:
+                    sent(g, "ag", (s - 1) * step)
                 item["slot"].append((room, step))
                 room += s * step
                 left = left // s
             item["fw"] = sems
-            sems += sizes[0]
+            sems += 1
+            sent(g, "fw", n * q)
             pieces.append(item)
             done = upto
-    return pieces, sems, room, total * n * nd
+    return pieces, sems, room, total * n * nd, out
 
 
 def kernel(
     nx,
     ny,
     nd,
+    feat_in,
+    cot_in,
+    w1_in,
+    w2_in,
+    nb,
+    count,
+    out_hbm,
+    gin_hbm,
+    gw1_hbm,
+    gw2_hbm,
     feat,
     cot,
     w1,
     w2,
-    nb,
-    count,
     out_ref,
     gin_ref,
-    gw1_ref,
-    gw2_ref,
+    load_sem,
+    save_sem,
     fld,
     rx,
     ry,
@@ -132,36 +173,66 @@
             return ry.at[f, (dy + 1) // 2]
         return rc.at[f, (dx + 1) // 2 * 2 + (dy + 1) // 2]
 
-    def desc(f, k):
+    late = 2 * (pairs - 2)
+
+    def desc(f, k, part=None):
         dx, dy = DIRS[k]
         far_x = edge - 1 if dx > 0 else 0
         far_y = edge - 1 if dy > 0 else 0
+        dst = halo_ref(f, -dx, -dy)
+        wait = k
         if dy == 0:
             src = fld.at[f, far_x]
         elif dx == 0:
             src = fld.at[f, :, far_y]
+            if part is not None:
+                lo, hi = part
+                src = fld.at[f, lo:hi, far_y]
+                dst = dst.at[lo:hi]
+                if lo == late:
+                    wait = len(DIRS) + (dy + 1) // 2
         else:
             src = fld.at[f, far_x, far_y]
         return pltpu.make_async_remote_copy(
             src_ref=src,
-            dst_ref=halo_ref(f, -dx, -dy),
+            dst_ref=dst,
             send_sem=send_sem.at[f, k],
-            recv_sem=recv_sem.at[f, k],
+            recv_sem=recv_sem.at[f, wait],
             device_id=peer(dx, dy),
             device_id_type=pl.DeviceIdType.MESH,
         )
 
-    def send(f):
+    def send(f, keep=lambda dx, dy: True, part=None):
         for k, (dx, dy) in enumerate(DIRS):
-            @pl.when(there(dx, dy))
-            def _(k=k):
-                desc(f, k).start()
-
-    def arrive(f):
+            if keep(dx, dy):
+                @pl.when(there(dx, dy))
+                def _(k=k):
+                    desc(f, k, part).start()
+
+    def arrive(f, keep=lambda dx, dy: True):
         for k, (dx, dy) in enumerate(DIRS):
-            @pl.when(there(-dx, -dy))
-            def _(k=k):
-                desc(f, k).wait_recv()
+            if keep(dx, dy):
+                @pl.when(there(-dx, -dy))
+                def _(k=k):
+                    desc(f, k).wait_recv()
+
+    def side_y(dx, dy):
+        return dx == 0
+
+    def arrive_y(f, part, lo, hi):
+        for k, (dx, dy) in enumerate(DIRS):
+            if dx == 0:
+                @pl.when(there(-dx, -dy))
+                def _(k=k, dy=dy):
+                    here = halo_ref(f, 0, -dy).at[lo:hi]
+                    pltpu.make_async_remote_copy(
+                        src_ref=here,
+                        dst_ref=here,
+                        send_sem=send_sem.at[f, k],
+                        recv_sem=recv_sem.at[f, len(DIRS) + (dy + 1) // 2 if part else k],
+                        device_id=peer(0, dy),
+                        device_id_type=pl.DeviceIdType.MESH,
+                    ).wait_recv()
 
     def drain(f):
         for k, (dx, dy) in enumerate(DIRS):
@@ -191,49 +262,63 @@
 
         lax.fori_loop(0, edge, body, 0)
 
-    def outer(f, pc):
+    def outer_x(f, pc):
         for h in range(2):
             x = 0 if h == 0 else edge + 1
             line(pc, x, sel[6 * h + 1], [rx[f, h, y] for y in range(edge)])
             for g in range(2):
                 yp = 0 if g == 0 else edge + 1
                 put(pc, x, yp, jnp.dot(sel[6 * h + 2 * g], rc[f, h * 2 + g], preferred_element_type=F32))
-            cat = jnp.concatenate([ry[f, h, x] for x in range(edge)], axis=1)
+
+    def outer_y(f, pc, xs):
+        for h in range(2):
+            cat = jnp.concatenate([ry[f, h, x] for x in xs], axis=1)
             got = jnp.dot(sel[3 + 2 * h], cat, preferred_element_type=F32)
-            for x in range(edge):
-                put(pc, x + 1, 0 if h == 0 else edge + 1, got[:, x * ch : (x + 1) * ch])
-
-    def conv(pc, w, use, hooks=None):
-        def body(i, carry):
-            left = None
-            right = None
-            for p in range(4):
-                lhs = pc[2 * i + p].reshape(plane, 9 * ch)
-                wl = w[9 * p : 9 * p + 9].reshape(9 * ch, ch) if p < 3 else None
-                wr = w[9 * p - 9 : 9 * p].reshape(9 * ch, ch) if p > 0 else None
-                if wr is None:
-                    left = jnp.dot(lhs, wl, preferred_element_type=F32)
-                elif wl is None:
-                    right = right + jnp.dot(lhs, wr, preferred_element_type=F32)
-                else:
-                    both = jnp.dot(lhs, jnp.concatenate([wl, wr], axis=1), preferred_element_type=F32)
-                    left = left + both[:, :ch]
-                    right = both[:, ch:] if right is None else right + both[:, ch:]
+            for n_x, x in enumerate(xs):
+                put(pc, x + 1, 0 if h == 0 else edge + 1, got[:, n_x * ch : (n_x + 1) * ch])
+
+    def outer(f, pc):
+        outer_x(f, pc)
+        outer_y(f, pc, range(edge))
+
+    def conv(pc, w, use, hooks=None, turn=0):
+        def body(step, carry):
+            i = lax.rem(step + turn, pairs) if turn else step
+
+            def lhs(p):
+                return pc[2 * i + p].reshape(plane, 9 * ch)
+
+            def tap(a):
+                return w[9 * a : 9 * a + 9].reshape(9 * ch, ch)
+
+            low = jnp.concatenate([tap(1), tap(0)], axis=1)
+            high = jnp.concatenate([tap(2), tap(1)], axis=1)
+            both = jnp.dot(
+                jnp.concatenate([lhs(1), lhs(2)], axis=1),
+                jnp.concatenate([low, high], axis=0),
+                preferred_element_type=F32,
+            )
+            left = both[:, :ch] + jnp.dot(lhs(0), tap(0), preferred_element_type=F32)
+            right = both[:, ch:] + jnp.dot(lhs(3), tap(2), preferred_element_type=F32)
             use(i, 0, left)
             use(i, 1, right)
-            hooked(i, hooks)
+            hooked(step, hooks)
             return carry
 
         lax.fori_loop(0, pairs, body, 0)
 
     def keep_t(i, h, v):
-        gt[h * ch : (h + 1) * ch, pl.ds(pl.multiple_of(i * plane, plane), plane)] = v.T.astype(BF16)
-
-    def tap_out(g, a, b, v):
+        t = v.T.astype(BF16)
+        for a in range(3):
+            at = pl.multiple_of((2 * i + h + a) * plane, plane)
+            gt[a * ch : (a + 1) * ch, pl.ds(at, plane)] = t
+
+    def tap_out(g, j, wide, v):
         per = ch // UNIT
-        for c in range(3):
-            t = v[:, c * ch : (c + 1) * ch].T.astype(BF16).reshape(per, UNIT, ch)
-            gb[g, pl.ds(((b * 3 + a) * 3 + c) * per, per)] = t
+        for s in range(wide):
+            for a in range(3):
+                t = v[a][:, s * ch : (s + 1) * ch].T.astype(BF16).reshape(per, UNIT, ch)
+                gb[g, pl.ds(((2 * j + s) * 3 + a) * per, per)] = t
 
     def hooked(i, hooks):
         for at, fns in sorted((hooks or {}).items()):
@@ -242,37 +327,40 @@
                 for fn in fns:
                     fn()
 
+    def taps(pc, g, j, wide):
+        lanes = pl.ds(pl.multiple_of(j * (2 * ch), 2 * ch), wide * ch)
+
+        def part(lo, hi, x0, x1):
+            rhs = pc[x0:x1, :, :, lanes].reshape((x1 - x0) * plane, wide * ch)
+            lhs = gt[lo * ch : hi * ch, x0 * plane : x1 * plane]
+            return jnp.dot(lhs, rhs, preferred_element_type=F32)
+
+        mid = part(0, 3, 2, edge)
+        low = part(0, 2, 1, 2)
+        high = part(1, 3, edge, edge + 1)
+        rows3 = (
+            mid[:ch] + low[:ch] + part(0, 1, 0, 1),
+            mid[ch : 2 * ch] + low[ch:] + high[:ch],
+            mid[2 * ch :] + high[ch:] + part(2, 3, edge + 1, edge + 2),
+        )
+        tap_out(g, j, wide, rows3)
+
     def wgrad(pc, g, hooks):
-        def body(b, carry):
-            lanes = pl.ds(pl.multiple_of(b * (3 * ch), 3 * ch), 3 * ch)
-            part = None
-            for p in range(4):
-                acc = None
-                for i in range(pairs):
-                    rhs = pc[2 * i + p, :, :, lanes].reshape(plane, 3 * ch)
-                    lhs = gt[:, i * plane : (i + 1) * plane]
-                    if p == 0:
-                        lhs = lhs[:ch]
-                    elif p == 3:
-                        lhs = lhs[ch:]
-                    t = jnp.dot(lhs, rhs, preferred_element_type=F32)
-                    acc = t if acc is None else acc + t
-                if p == 3:
-                    tap_out(g, 2, b, part + acc)
-                elif p > 0:
-                    tap_out(g, p - 1, b, part + acc[ch:])
-                if p < 3:
-                    part = acc[:ch]
-            hooked(b, hooks)
+        def body(j, carry):
+            taps(pc, g, j, 2)
+            hooked(j, hooks)
             return carry
 
-        lax.fori_loop(0, 3, body, 0)
+        lax.fori_loop(0, 4, body, 0)
+        taps(pc, g, 4, 1)
+        run(hooks.get(4, []))
 
     n = nx * ny
     core = lax.axis_index("dp")
     me = ix * ny + iy
     mesh_id = pl.DeviceIdType.MESH
-    pieces, _, _, units = layout(nx, ny, nd, ch)
+    pieces, _, _, units, sent = layout(nx, ny, nd, ch)
+    kinds = ("pair", "rs", "ag", "fw")
     side = side_of(ny)
 
     def each(lo, hi, fn):
@@ -305,10 +393,13 @@
                 self.coords = (first, second, ix)
                 self.other = second
                 self.steps = (1 + core * (side - 1), side - core * (side - 1))
-            else:
+            elif m == 2:
                 self.coords = (iy, ix)
                 self.other = iy
                 self.steps = (1,)
+            else:
+                self.coords = (me,)
+                self.other = me
             self.size = [n * q]
             self.off = [0]
             for l in range(m):
@@ -322,6 +413,8 @@
         def to(self, l, o):
             c = self.coords[l]
             p = lax.rem(c + o, self.sizes[l])
+            if self.m == 1:
+                return p, group(p)
             if l == self.m - 1:
                 return p, {"sx": p}
             return p, {"sy": iy + (p - c) * self.steps[l]}
@@ -329,11 +422,11 @@
         def frm(self, l, o):
             return lax.rem(self.coords[l] + self.sizes[l] - o, self.sizes[l])
 
-        def copy(self, src, dst, k, dev):
+        def copy(self, src, dst, kind, k, dev):
             return pltpu.make_async_remote_copy(
                 src_ref=src,
                 dst_ref=dst,
-                send_sem=sum_send.at[k],
+                send_sem=sum_send.at[4 * self.g + kinds.index(kind)],
                 recv_sem=sum_recv.at[k],
                 device_id=dev,
                 device_id_type=mesh_id,
@@ -343,6 +436,7 @@
             return self.copy(
                 gb.at[self.g, pl.ds(self.theirs, self.size[0])],
                 dx_buf.at[self.g, pl.ds(self.hb, self.size[0])],
+                "pair",
                 self.it["pair"],
                 {"dp": 1 - core},
             )
@@ -357,20 +451,34 @@
             return self.copy(
                 hs.at[self.g, pl.ds(self.hb + at, step)],
                 rb.at[pl.ds(room + o * step, step)],
-                self.it["rs"][l] + o,
+                "rs",
+                self.it["rs"][l],
                 dev,
             )
+
+        def rs_wait(self, l):
+            room, step = self.it["slot"][l]
+            _, dev = self.to(l, 1)
+            here = rb.at[pl.ds(room + step, (self.sizes[l] - 1) * step)]
+            self.copy(here, here, "rs", self.it["rs"][l], dev).wait_recv()
 
         def ag(self, l, o, owner):
             _, dev = self.to(l, o)
             size = self.size[l + 1]
             here = pl.ds(self.mine + self.off[l] + owner * size, size)
-            return self.copy(fin.at[self.g, here], fin.at[self.g, here], self.it["ag"][l] + o, dev)
+            k = self.it["ag"][l] + (o if l == 0 else 0)
+            return self.copy(fin.at[self.g, here], fin.at[self.g, here], "ag", k, dev)
+
+        def ag_wait(self, l):
+            size = self.size[l + 1]
+            _, dev = self.to(l, 1)
+            here = fin.at[self.g, pl.ds(self.mine + self.off[l], (self.sizes[l] - 1) * size)]
+            self.copy(here, here, "ag", self.it["ag"][l], dev).wait_recv()
 
         def fw(self, o, base, c):
             size = self.size[1]
             here = pl.ds(base + lax.rem(c + self.sizes[0] - o, self.sizes[0]) * size, size)
-            return self.copy(fin.at[self.g, here], fin.at[self.g, here], self.it["fw"] + o, {"dp": 1 - core})
+            return self.copy(fin.at[self.g, here], fin.at[self.g, here], "fw", self.it["fw"], {"dp": 1 - core})
 
         def begin(self):
             self.pair().start()
@@ -396,7 +504,7 @@
             if l < 0:
                 self.pair().wait_recv()
             else:
-                each(1, self.sizes[l], lambda o: self.rs(l, o).wait_recv())
+                self.rs_wait(l)
             nxt = l + 1
             if nxt == self.m:
                 size = self.size[self.m]
@@ -425,7 +533,7 @@
 
         def settle(self):
             l = self.m - 1
-            each(1, self.sizes[l], lambda o: self.rs(l, o).wait_recv())
+            self.rs_wait(l)
             room, step = self.it["slot"][l]
 
             def part(p):
@@ -446,17 +554,20 @@
                 self.fw(0, self.mine, self.coords[0]).start()
 
         def gather(self, l):
+            if l > 0:
+                self.ag_wait(l)
+                self.share(l - 1)
+                return
+
             def one(o):
                 self.ag(l, o, self.frm(l, o)).wait_recv()
-                if l == 0:
-                    self.fw(o, self.mine, self.coords[0]).start()
+                self.fw(o, self.mine, self.coords[0]).start()
 
             each(1, self.sizes[l], one)
-            if l > 0:
-                self.share(l - 1)
 
         def arrive(self):
-            each(0, self.sizes[0], lambda o: self.fw(o, self.theirs, self.other).wait_recv())
+            here = fin.at[self.g, pl.ds(self.theirs, self.size[0])]
+            self.copy(here, here, "fw", self.it["fw"], {"dp": 1 - core}).wait_recv()
 
         def stages(self):
             out = [self.begin]
@@ -469,41 +580,38 @@
             out.append(self.arrive)
             return out
 
-        def drain(self):
-            self.pair().wait_send()
-            for l in range(self.m):
-                each(1, self.sizes[l], lambda o: self.rs(l, o).wait_send())
-                if not self.last(l):
-                    each(1, self.sizes[l], lambda o: self.ag(l, o, self.coords[l]).wait_send())
-            each(0, self.sizes[0], lambda o: self.fw(o, self.mine, self.coords[0]).wait_send())
-
     sums = [Sum(item) for item in pieces]
     queue = {(s.g, s.it["b"]): s.stages() for s in sums}
 
-    listed = set()
-
-    def adv(g, b, s):
-        listed.add((g, b, s))
-
-        def run():
-            if s < len(queue.get((g, b), [])):
-                queue[g, b][s]()
-
-        return run
+    points = {}
+    for s in sums:
+        k = (s.g, s.it["b"])
+        names = STEPS[k]
+        for at, fn in enumerate(queue[k]):
+            points.setdefault(names[at] if at < len(names) else "end", []).append((at, fn))
+
+    def at(name):
+        return [fn for _, fn in points.get(name, [])]
+
+    def hooks_of(name, count):
+        return {i: at(name + "." + str(i)) for i in range(count) if at(name + "." + str(i))}
+
+    def run(fns):
+        for fn in fns:
+            fn()
 
     def finish(g, ref):
         per = ch // UNIT
         for k in range(27):
             a, b, c = k // 9, k // 3 % 3, k % 3
-            j = (b * 3 + a) * 3 + c
-            ref[k * per : (k + 1) * per] = fin[g, j * per : (j + 1) * per]
-
-    for dx, dy in DIRS:
-        @pl.when(jnp.logical_not(there(dx, dy)))
-        def _(dx=dx, dy=dy):
-            for f in range(4):
-                r = halo_ref(f, dx, dy)
-                r[...] = jnp.zeros(r.shape, BF16)
+            j = (b * 3 + c) * 3 + a
+            pltpu.make_async_copy(
+                fin.at[g, j * per : (j + 1) * per], ref.at[k * per : (k + 1) * per], save_sem.at[2 + g]
+            ).start()
+
+    def finished(g, ref):
+        count = 27 * (ch // UNIT)
+        pltpu.make_async_copy(fin.at[g, 0:count], ref.at[0:count], save_sem.at[2 + g]).wait()
 
     barrier = pltpu.get_barrier_semaphore()
     each(
@@ -514,6 +622,20 @@
         ),
     )
     pl.semaphore_signal(barrier, inc=1, device_id={"dp": 1 - core}, device_id_type=mesh_id)
+
+    loads = [
+        pltpu.make_async_copy(a, b, load_sem.at[s])
+        for s, (a, b) in enumerate(((feat_in, feat), (w2_in, w2), (w1_in, w1), (cot_in, cot)))
+    ]
+    for load in loads:
+        load.start()
+
+    for dx, dy in DIRS:
+        @pl.when(jnp.logical_not(there(dx, dy)))
+        def _(dx=dx, dy=dy):
+            for f in range(4):
+                r = halo_ref(f, dx, dy)
+                r[...] = jnp.zeros(r.shape, BF16)
 
     spare = units - 27 * (ch // UNIT)
     if spare:
@@ -553,6 +675,7 @@
         fld[0, x] = v.astype(BF16).reshape(edge, rows, ch)
         return carry
 
+    loads[0].wait()
     lax.fori_loop(0, edge, mask_in, 0)
 
     pl.semaphore_wait(barrier, n)
@@ -562,7 +685,9 @@
 
     send(0)
     inner(0, pc_a)
+    loads[1].wait()
     flip(w2, w2f)
+    loads[2].wait()
     arrive(0)
     outer(0, pc_a)
 
@@ -571,12 +696,28 @@
         pre[x] = v
         store(1, x, v * jax.nn.sigmoid(v) * live[...])
 
-    conv(pc_a, w1, use1)
-    send(1)
+    def halo_1(i, dx):
+        def go():
+            if dx:
+                send(1, lambda x, y: x == dx)
+            send(1, side_y, (2 * i, 2 * i + 2))
+
+        return [go]
+
+    last = pairs - 1
+    hooks = {(i + 1) % pairs: halo_1(i, {0: -1, last: 1}.get(i, 0)) for i in range(pairs)}
+    conv(pc_a, w1, use1, hooks, last)
     inner(1, pc_b)
     flip(w1, w1f)
-    arrive(1)
-    outer(1, pc_b)
+    arrive(1, lambda x, y: x != 0)
+    arrive_y(1, False, 0, edge - 2)
+    outer_x(1, pc_b)
+    outer_y(1, pc_b, [x for x in range(edge) if x not in (late, late + 1)])
+    loads[3].wait()
+
+    def rest_1():
+        arrive_y(1, True, late, late + 2)
+        outer_y(1, pc_b, [late, late + 1])
 
     def use2(i, h, v):
         x = 2 * i + h
@@ -587,38 +728,15 @@
         store(2, x, g)
         keep_t(i, h, g)
 
-    AT = {
-        "w2": {0: [adv(0, 0, 0)], 1: [adv(0, 1, 0), adv(0, 0, 1)], 2: [adv(0, 2, 0), adv(0, 1, 1)]},
-        "o2": [adv(0, 2, 1)],
-        "c3": {
-            0: [adv(0, 0, 2)],
-            1: [adv(0, 1, 2)],
-            2: [adv(0, 2, 2), adv(0, 0, 3)],
-            3: [adv(0, 1, 3)],
-        },
-        "w1": {
-            0: [adv(1, 0, 0), adv(0, 2, 3)],
-            1: [adv(1, 1, 0), adv(1, 0, 1), adv(0, 0, 4), adv(0, 1, 4)],
-            2: [adv(1, 2, 0), adv(1, 1, 1), adv(0, 2, 4)],
-        },
-        "o3": [adv(1, 2, 1), adv(1, 0, 2)],
-        "c4": {
-            0: [adv(1, 1, 2), adv(0, 0, 5)],
-            1: [adv(1, 2, 2), adv(0, 1, 5)],
-            2: [adv(0, 2, 5), adv(0, 0, 6), adv(1, 0, 3)],
-            3: [adv(0, 1, 6), adv(0, 2, 6), adv(1, 1, 3)],
-        },
-        "end": [adv(0, 0, 7), adv(0, 1, 7), adv(1, 2, 3), adv(1, 0, 4), adv(0, 2, 7), adv(1, 1, 4), adv(0, 0, 8), adv(1, 2, 4)],
-    }
-
-    conv(pc_b, w2, use2)
+    conv(pc_b, w2, use2, {0: [rest_1]})
+    save_out = pltpu.make_async_copy(out_ref, out_hbm, save_sem.at[0])
+    save_out.start()
     send(2)
     inner(2, pc_c)
-    wgrad(pc_b, 0, AT["w2"])
+    wgrad(pc_b, 0, hooks_of("w2", 5))
     arrive(2)
     outer(2, pc_c)
-    for fn in AT["o2"]:
-        fn()
+    run(at("o2"))
 
     def use3(i, h, v):
         x = 2 * i + h
@@ -626,33 +744,42 @@
         store(3, x, g)
         keep_t(i, h, g)
 
-    conv(pc_c, w2f, use3, AT["c3"])
+    conv(pc_c, w2f, use3, hooks_of("c3", pairs))
     send(3)
-    wgrad(pc_a, 1, AT["w1"])
+    wgrad(pc_a, 1, hooks_of("w1", 5))
     inner(3, pc_c)
     arrive(3)
     outer(3, pc_c)
-    for fn in AT["o3"]:
-        fn()
+    run(at("o3"))
 
     def use4(i, h, v):
         x = 2 * i + h
         g = (fld[2, x].reshape(plane, ch).astype(F32) + v) * live[...]
         gin_ref[x] = g.astype(BF16).reshape(edge, rows, ch)
 
-    conv(pc_c, w1f, use4, AT["c4"])
-    for fn in AT["end"]:
+    conv(pc_c, w1f, use4, hooks_of("c4", pairs))
+    save_gin = pltpu.make_async_copy(gin_ref, gin_hbm, save_sem.at[1])
+    save_gin.start()
+    for _, fn in sorted(points.get("end", []), key=lambda e: e[0]):
         fn()
-    for k, todo in queue.items():
-        for s, fn in enumerate(todo):
-            if k + (s,) not in listed:
-                fn()
-    finish(0, gw2_ref)
-    finish(1, gw1_ref)
+    finish(0, gw2_hbm)
+    finish(1, gw1_hbm)
+    save_out.wait()
+    save_gin.wait()
+    finished(0, gw2_hbm)
+    finished(1, gw1_hbm)
     for f in range(4):
         drain(f)
-    for s in sums:
-        s.drain()
+    for (g, kind), count in sent.items():
+        here = gb.at[g, pl.ds(0, count)]
+        pltpu.make_async_remote_copy(
+            src_ref=here,
+            dst_ref=here,
+            send_sem=sum_send.at[4 * g + kinds.index(kind)],
+            recv_sem=sum_recv.at[0],
+            device_id={"dp": 1 - core},
+            device_id_type=mesh_id,
+        ).wait_send()
 
 
 def shards(nx, ny, nd, features, cotangent, first_weight, second_weight, neighbours, counts):
@@ -661,17 +788,25 @@
     plane = edge * rows
     flat = (edge, edge, rows, ch)
     scale = float(nx * ny * nd * slots * edge**3) ** -0.5
-    vmem = pl.BlockSpec(memory_space=pltpu.VMEM)
+    hbm = pl.BlockSpec(memory_space=pl.ANY)
     smem = pl.BlockSpec(memory_space=pltpu.SMEM)
-    _, nsem, room, units = layout(nx, ny, nd, ch)
+    _, nsem, room, units, _ = layout(nx, ny, nd, ch)
     gshape = jax.ShapeDtypeStruct((units, UNIT, ch), BF16)
     fshape = jax.ShapeDtypeStruct(flat, BF16)
     out, gin, g1, g2 = pl.pallas_call(
         functools.partial(kernel, nx, ny, nd),
         out_shape=[fshape, fshape, gshape, gshape],
-        in_specs=[vmem] * 4 + [smem] * 2,
-        out_specs=[vmem] * 4,
+        in_specs=[hbm] * 4 + [smem] * 2,
+        out_specs=[hbm] * 4,
         scratch_shapes=[
+            pltpu.VMEM(flat, BF16),
+            pltpu.VMEM(flat, BF16),
+            pltpu.VMEM((27, ch, ch), BF16),
+            pltpu.VMEM((27, ch, ch), BF16),
+            pltpu.VMEM(flat, BF16),
+            pltpu.VMEM(flat, BF16),
+            pltpu.SemaphoreType.DMA((4,)),
+            pltpu.SemaphoreType.DMA((4,)),
             pltpu.VMEM((4,) + flat, BF16),
             pltpu.VMEM((4, 2, edge, rows, ch), BF16),
             pltpu.VMEM((4, 2, edge, rows, ch), BF16),
@@ -680,9 +815,9 @@
             pltpu.VMEM((edge + 2, edge, rows, 9 * ch), BF16),
             pltpu.VMEM((edge + 2, edge, rows, 9 * ch), BF16),
             pltpu.VMEM((edge, plane, ch), F32),
-            pltpu.VMEM((2 * ch, edge // 2 * plane), BF16),
+            pltpu.VMEM((3 * ch, (edge + 2) * plane), BF16),
             pltpu.SemaphoreType.DMA((4, len(DIRS))),
-            pltpu.SemaphoreType.DMA((4, len(DIRS))),
+            pltpu.SemaphoreType.DMA((4, len(DIRS) + 2)),
             pltpu.VMEM((27, ch, ch), BF16),
             pltpu.VMEM((27, ch, ch), BF16),
             pltpu.VMEM((9, 3 * rows, rows), BF16),
@@ -692,7 +827,7 @@
             pltpu.VMEM((2, units // nd, UNIT, ch), BF16),
             pltpu.VMEM((room, UNIT, ch), BF16),
             pltpu.VMEM((2, units, UNIT, ch), BF16),
-            pltpu.SemaphoreType.DMA((nsem,)),
+            pltpu.SemaphoreType.DMA((8,)),
             pltpu.SemaphoreType.DMA((nsem,)),
         ],
         compiler_params=pltpu.CompilerParams(

time: 72 us -> 65.8 us (0.914)
  Pallas kernels: 65.3 us -> 59.1 us
    pallas_call x1, Pallas kernels: 65.3 us -> 59.1 us  [shards(): pl.pallas_call(functools.partial(kernel, nx, ny, nd), out_shape=[fshape,...]
where the time goes in v2:
time: 65.8 us; the launch traced here: 65.6 us
  Pallas kernels  59.1 us (90%)
  other arithmetic  3.59 us (5%)
  local copies, waits for them, and re-layouts  1.59 us (2%)
  between operations  1.3 us (2%)
    pallas_call x1, Pallas kernels, shards(): pl.pallas_call(functools.partial(kernel, nx, ny, nd), out_shape=[fshape,...  59.1 us
    mul x1, other arithmetic, finish(): return g.reshape(27, ch, ch).astype(F32) * scale  3.59 us
    unnamed x6, local copies, waits for them, and re-layouts  1.59 us

profile of v2, /device:TPU:1, one launch (start us, length us, event | category | flops | bytes accessed | tf_op | source)
XLA Modules:
  0.0 65.6 jit_solution(12833541639752008532)
XLA Ops:
  1.3 59.1 %shard_map.93 = (bf16[8,8,32,128]{3,2,1,0:T(8,128)(2,1)}, bf16[8,8,32,128]{3,2,1,0:T(8,128)(2,1)}, bf16[224,16,128]{2,1,0:T(8,128)(2,1)}, bf16[224,16,128]{2,1,0:T(8,128)(2,1)}) custom-call(bf16[8,8,32,128]{3,2,1,0:T(8,128)(2,1)} %bitcast.13, bf16[8,8,32,128]{3,2,1,0:T(8,128)(2,1)} %bitcast.14, bf16[27,128,128]{2,1,0:T(8,128)(2,1)} %w1_in.1, ...), custom_call_target="tpu_custom_call" | custom-call | tf_op jit(solution)/shard_map/pallas_call | solution.py:796
  60.4 0.0 copy-start.1
  60.4 0.0 copy-start
  60.4 3.6 %convert_multiply_fusion = (f32[216,16,128]{2,1,0:T(8,128)}, f32[216,16,128]{2,1,0:T(8,128)}) fusion(bf16[224,16,128]{2,1,0:T(8,128)(2,1)} %get-tuple-element.11, bf16[224,16,128]{2,1,0:T(8,128)(2,1)} %get-tuple-element.10), kind=kLoop, calls=%fused_computation | loop fusion | flops 1769472 | bytes 5308416 | tf_op jit(solution)/shard_map/mul | solution.py:846
  64.0 0.0 copy-done.1
  64.0 0.8 %copy.13 = bf16[1,8,8,4,8,128]{5,4,3,2,1,0:T(8,128)(2,1)} copy(bf16[1,8,8,4,8,128]{5,4,3,2,1,0:T(8,128)(2,1)S(1)} %bitcast.12) | data formatting | bytes 1048576
  64.8 0.0 copy-done
  64.8 0.8 %copy.14 = bf16[1,8,8,4,8,128]{5,4,3,2,1,0:T(8,128)(2,1)} copy(bf16[1,8,8,4,8,128]{5,4,3,2,1,0:T(8,128)(2,1)S(1)} %bitcast.11) | data formatting | bytes 1048576
Async XLA Ops:
  60.4 3.6 %copy-start.1 = (bf16[8,8,32,128]{3,2,1,0:T(8,128)(2,1)S(1)}, bf16[8,8,32,128]{3,2,1,0:T(8,128)(2,1)}, u32[]{:S(2)}) copy-start(bf16[8,8,32,128]{3,2,1,0:T(8,128)(2,1)} %get-tuple-element.8) | copy-start | bytes 1572868
  60.4 4.4 %copy-start = (bf16[8,8,32,128]{3,2,1,0:T(8,128)(2,1)S(1)}, bf16[8,8,32,128]{3,2,1,0:T(8,128)(2,1)}, u32[]{:S(2)}) copy-start(bf16[8,8,32,128]{3,2,1,0:T(8,128)(2,1)} %get-tuple-element.9) | copy-start | bytes 1572868

commit v3 on v2

--- a/solution.py
+++ b/solution.py
@@ -20,19 +20,19 @@
 
 MODES = (
     ("yz", "yz", "yz", "yz", "yz"),
-    ("yz", "yz", "yzw", "yzw", "yzw"),
+    ("yz", "yz", "yz", "yzw", "yzw"),
 )
 STEPS = {
-    (0, 0): ("w2.0", "w2.2", "c3.3", "w1.4", "c4.2",),
-    (0, 1): ("w2.1", "w2.3", "c3.3", "w1.4", "c4.2",),
-    (0, 2): ("w2.2", "w2.4", "c3.3", "w1.4", "c4.2",),
-    (0, 3): ("w2.3", "o2", "w1.0", "o3", "c4.2",),
-    (0, 4): ("w2.4", "c3.0", "w1.1", "o3", "c4.2",),
-    (1, 0): ("w1.0", "w1.2", "c4.1",),
-    (1, 1): ("w1.1", "w1.3", "c4.1",),
-    (1, 2): ("w1.2", "w1.4", "c4.1",),
-    (1, 3): ("w1.3", "o3", "c4.3",),
-    (1, 4): ("w1.4", "o3", "c4.3",),
+    (0, 0): ("w2.0", "w2.2", "c3.3", "w1.4", "c4.2"),
+    (0, 1): ("w2.1", "w2.3", "c3.3", "w1.4", "c4.2"),
+    (0, 2): ("w2.2", "w2.4", "c3.3", "w1.4", "c4.2"),
+    (0, 3): ("w2.3", "o2", "w1.0", "o3", "c4.2"),
+    (0, 4): ("w2.4", "c3.0", "w1.1", "o3", "c4.2"),
+    (1, 0): ("w1.0", "w1.2", "c4.1"),
+    (1, 1): ("w1.1", "w1.3", "c4.1"),
+    (1, 2): ("w1.2", "w1.4", "c4.1"),
+    (1, 3): ("w1.3", "o3", "c4.3"),
+    (1, 4): ("w1.4", "o3", "c4.3"),
 }
 
 

time: 65.8 us -> 65.6 us (level)
  no operation moved by 1% of the time
where the time goes in v3:
time: 65.6 us; the launch traced here: 65.4 us
  Pallas kernels  58.9 us (90%)
  other arithmetic  3.59 us (5%)
  local copies, waits for them, and re-layouts  1.59 us (2%)
  between operations  1.3 us (2%)
    pallas_call x1, Pallas kernels, shards(): pl.pallas_call(functools.partial(kernel, nx, ny, nd), out_shape=[fshape,...  58.9 us
    mul x1, other arithmetic, finish(): return g.reshape(27, ch, ch).astype(F32) * scale  3.59 us
    unnamed x6, local copies, waits for them, and re-layouts  1.59 us

profile of v3, /device:TPU:1, one launch (start us, length us, event | category | flops | bytes accessed | tf_op | source)
XLA Modules:
  0.0 65.4 jit_solution(9544726974366559168)
XLA Ops:
  1.3 58.9 %shard_map.93 = (bf16[8,8,32,128]{3,2,1,0:T(8,128)(2,1)}, bf16[8,8,32,128]{3,2,1,0:T(8,128)(2,1)}, bf16[224,16,128]{2,1,0:T(8,128)(2,1)}, bf16[224,16,128]{2,1,0:T(8,128)(2,1)}) custom-call(bf16[8,8,32,128]{3,2,1,0:T(8,128)(2,1)} %bitcast.13, bf16[8,8,32,128]{3,2,1,0:T(8,128)(2,1)} %bitcast.14, bf16[27,128,128]{2,1,0:T(8,128)(2,1)} %w1_in.1, ...), custom_call_target="tpu_custom_call" | custom-call | tf_op jit(solution)/shard_map/pallas_call | solution.py:796
  60.2 0.0 copy-start.1
  60.2 0.0 copy-start
  60.2 3.6 %convert_multiply_fusion = (f32[216,16,128]{2,1,0:T(8,128)}, f32[216,16,128]{2,1,0:T(8,128)}) fusion(bf16[224,16,128]{2,1,0:T(8,128)(2,1)} %get-tuple-element.11, bf16[224,16,128]{2,1,0:T(8,128)(2,1)} %get-tuple-element.10), kind=kLoop, calls=%fused_computation | loop fusion | flops 1769472 | bytes 5308416 | tf_op jit(solution)/shard_map/mul | solution.py:846
  63.8 0.0 copy-done.1
  63.8 0.8 %copy.13 = bf16[1,8,8,4,8,128]{5,4,3,2,1,0:T(8,128)(2,1)} copy(bf16[1,8,8,4,8,128]{5,4,3,2,1,0:T(8,128)(2,1)S(1)} %bitcast.12) | data formatting | bytes 1048576
  64.6 0.0 copy-done
  64.6 0.8 %copy.14 = bf16[1,8,8,4,8,128]{5,4,3,2,1,0:T(8,128)(2,1)} copy(bf16[1,8,8,4,8,128]{5,4,3,2,1,0:T(8,128)(2,1)S(1)} %bitcast.11) | data formatting | bytes 1048576
Async XLA Ops:
  60.2 3.6 %copy-start.1 = (bf16[8,8,32,128]{3,2,1,0:T(8,128)(2,1)S(1)}, bf16[8,8,32,128]{3,2,1,0:T(8,128)(2,1)}, u32[]{:S(2)}) copy-start(bf16[8,8,32,128]{3,2,1,0:T(8,128)(2,1)} %get-tuple-element.8) | copy-start | bytes 1572868
  60.2 4.4 %copy-start = (bf16[8,8,32,128]{3,2,1,0:T(8,128)(2,1)S(1)}, bf16[8,8,32,128]{3,2,1,0:T(8,128)(2,1)}, u32[]{:S(2)}) copy-start(bf16[8,8,32,128]{3,2,1,0:T(8,128)(2,1)} %get-tuple-element.9) | copy-start | bytes 1572868
